TPU v7x, 32 devices: a whole 2x2x4 slice. The times are simulated.
32 devices in a mesh: view: 4 (over z), brick: 8 (over y, x, core).
Axes of the slice: x: 2, y: 2, z: 4, core: 2. Of those that a mesh axis runs over, the one named last changes fastest.
Arguments:
- estimate: float32 [16, 16, 64, 256], P('brick'), may hold values from 0.5 to 2
- views_data: bfloat16 [4, 8, 112, 32, 128], P('view', 'brick'), may hold values from 0.5 to 2
- psf_taps: float32 [4, 3, 31], P('view'), may hold values from 0.02 to 1
- seg_owner: int32 [4, 8, 32, 1], P('view', 'brick'), may hold values from 0 to 7; in each aligned block of 32 rows (0 to 31, 32 to 63, ..., all dimensions but the last counted through in order) at most 8 rows name the same one
- seg_local: int32 [4, 8, 32], P('view', 'brick'), may hold values from 0 to 1
- seg_offset: int32 [4, 8, 32], P('view', 'brick'), may hold values from 0 to 12
- seg_extent: int32 [4, 8, 32], P('view', 'brick'), may hold values from 1 to 4, 112 in all within a row
- view_shift: int32 [4, 2], P('view'), may hold values from 0 to 32
Outputs:
- joined: float32 [16, 16, 64, 256], P('brick')
Inputs may be any that keep to these rules, and one draw needn't show every extreme that they name: `seg_owner`: within one tile's 32 segments no owner is named more than 8 times, and in every draw some tile names one owner exactly 8 times. `seg_extent`: the 32 extents of a tile sum to 112, and some extent is exactly 4.
All inputs are finite; a program needn't handle non-finite values.
Results may differ from a plain program's by a relative error of at most 0.0003.
Values may be sent and summed in bfloat16 or wider, within the bound.
No kernel may reach another device: no remote copies, remote signals or barrier semaphores. Data moves between devices by JAX's collectives and lax.ppermute only.
A program may use at most 128 MiB of HBM per device.

v0:
```python
import jax
import jax.numpy as jnp
from jax import lax
from jax.sharding import PartitionSpec as P

ITERS = 2
EXTMAX = 4


def blur_matrix(tap_values, length):
    centre = tap_values.shape[0] // 2
    positions = jnp.arange(length, dtype=jnp.int32)
    offsets_tab = positions[:, None] - positions[None, :] + centre
    match_table = (
        offsets_tab[:, :, None] == jnp.arange(tap_values.shape[0], dtype=jnp.int32)[None, None, :]
    ).astype(tap_values.dtype)
    return jnp.sum(match_table * tap_values[None, None, :], axis=-1)


def apply_blur(volume, matrices):
    along_z, along_y, along_x = matrices
    highest = lax.Precision.HIGHEST
    volume = jnp.einsum("...xyz,zw->...xyw", volume, along_z, precision=highest)
    volume = jnp.einsum("...xyz,yw->...xwz", volume, along_y, precision=highest)
    volume = jnp.einsum("...xyz,xw->...wyz", volume, along_x, precision=highest)
    return volume


def view_matrices(view_taps, tile_x, tile_y, tile_z):
    normed = view_taps / jnp.sum(view_taps, axis=1, keepdims=True)
    forward = (
        blur_matrix(normed[2], tile_z),
        blur_matrix(normed[1], tile_y),
        blur_matrix(normed[0], tile_x),
    )
    backward = (forward[0].T, forward[1].T, forward[2].T)
    return (forward, backward)


def slot_ranks(owners):
    positions = jnp.arange(owners.shape[-1], dtype=jnp.int32)
    same_owner = owners[..., :, None] == owners[..., None, :]
    earlier = positions[None, :] < positions[:, None]
    return jnp.sum((same_owner & earlier).astype(jnp.int32), axis=-1)


def on_device(
    estimate, views_data, psf_taps, seg_owner, seg_local, seg_offset, seg_extent, view_shift
):
    per_owner, brick_x, brick_y, brick_z = estimate.shape
    tile_x, tile_y, tile_z = (views_data.shape[2], views_data.shape[3], views_data.shape[4])
    seg_count = seg_extent.shape[2]
    brick_count = lax.axis_size("brick")
    owner_me = lax.axis_index("brick")
    capacity = max(2, 2 * seg_count // brick_count)
    slot_rows = capacity * EXTMAX
    own_rows = per_owner * brick_x
    forward, backward = view_matrices(psf_taps[0], tile_x, tile_y, tile_z)
    shift_y = view_shift[0, 0]
    shift_z = view_shift[0, 1]
    measured = views_data[0, 0].astype(jnp.float32)
    lists = (
        lax.all_gather(seg_owner[:, :, :, 0], "brick", axis=1, tiled=True),
        lax.all_gather(seg_local, "brick", axis=1, tiled=True),
        lax.all_gather(seg_offset, "brick", axis=1, tiled=True),
        lax.all_gather(seg_extent, "brick", axis=1, tiled=True),
    )
    all_owner, all_local, all_offset, all_extent = (
        lists[0][0],
        lists[1][0],
        lists[2][0],
        lists[3][0],
    )
    own_owner = seg_owner[0, 0, :, 0]
    own_local = seg_local[0, 0]
    own_offset = seg_offset[0, 0]
    own_extent = seg_extent[0, 0]
    own_rank = slot_ranks(own_owner)
    seg_ids = jnp.arange(seg_count, dtype=jnp.int32)
    peer_ids = jnp.arange(brick_count, dtype=jnp.int32)
    slot_ids = jnp.arange(capacity, dtype=jnp.int32)
    row_steps = jnp.arange(EXTMAX, dtype=jnp.int32)
    starts = jnp.cumsum(own_extent) - own_extent
    tile_rows = jnp.arange(tile_x, dtype=jnp.int32)
    seg_of = jnp.sum((starts[None, :] <= tile_rows[:, None]).astype(jnp.int32), axis=1) - 1
    within = tile_rows - starts[seg_of]
    source_of_row = (
        (own_owner[seg_of] * per_owner + own_local[seg_of]) * brick_x + own_offset[seg_of] + within
    )
    back_match = (own_owner[None, None, :] == peer_ids[:, None, None]) & (
        own_rank[None, None, :] == slot_ids[None, :, None]
    )
    back_valid = jnp.any(back_match, axis=-1)
    back_seg = jnp.sum(back_match.astype(jnp.int32) * seg_ids, axis=-1)
    back_mask = back_valid[:, :, None] & (
        row_steps[None, None, :] < own_extent[back_seg][:, :, None]
    )
    back_rows = jnp.where(
        back_mask, starts[back_seg][:, :, None] + row_steps[None, None, :], 0
    ).reshape(-1)
    back_mask = back_mask.reshape(-1)
    all_rank = slot_ranks(all_owner)
    owner_match = (all_owner[:, None, :] == owner_me) & (
        all_rank[:, None, :] == slot_ids[None, :, None]
    )
    owner_valid = jnp.any(owner_match, axis=-1)
    owner_seg = jnp.sum(owner_match.astype(jnp.int32) * seg_ids, axis=-1)
    owner_base = jnp.take_along_axis(all_local, owner_seg, axis=1) * brick_x + jnp.take_along_axis(
        all_offset, owner_seg, axis=1
    )
    owner_ext = jnp.take_along_axis(all_extent, owner_seg, axis=1)
    owner_mask = owner_valid[:, :, None] & (row_steps[None, None, :] < owner_ext[:, :, None])
    owner_rows = jnp.where(
        owner_mask, owner_base[:, :, None] + row_steps[None, None, :], 0
    ).reshape(-1)
    owner_mask = owner_mask.reshape(-1)
    landing = (
        (owner_rows[None, :] == jnp.arange(own_rows, dtype=jnp.int32)[:, None])
        & owner_mask[None, :]
    ).astype(jnp.float32)

    def to_owners(projected):
        outgoing = jnp.where(back_mask[:, None, None], jnp.take(projected, back_rows, axis=0), 0.0)
        outgoing = outgoing.reshape(brick_count, slot_rows, tile_y, tile_z)
        arrived = lax.all_to_all(
            outgoing, "brick", split_axis=0, concat_axis=0, tiled=True
        ).reshape(-1, tile_y, tile_z)
        accumulated = jnp.einsum("pq,qyz->pyz", landing, arrived, precision=lax.Precision.HIGHEST)
        brick_part = lax.dynamic_update_slice(
            jnp.zeros((own_rows, brick_y, brick_z), jnp.float32), accumulated, (0, shift_y, shift_z)
        )
        brick_part = brick_part.reshape(per_owner, brick_x, brick_y, brick_z)
        return lax.psum(brick_part, "view")

    weight = to_owners(apply_blur(jnp.ones((tile_x, tile_y, tile_z), jnp.float32), backward))
    current = estimate
    for sweep in range(ITERS):
        flat_est = current.reshape(own_rows, brick_y, brick_z)
        cropped = lax.dynamic_slice(
            flat_est, (0, shift_y, shift_z), (own_rows, tile_y, tile_z)
        ).astype(jnp.bfloat16)
        gathered = lax.all_gather(cropped, "brick", axis=0, tiled=True)
        view_tile = jnp.take(gathered, source_of_row, axis=0)
        correction_view_tile = view_tile.astype(jnp.float32)
        quotient = measured / apply_blur(correction_view_tile, forward)
        correction = to_owners(apply_blur(quotient, backward))
        current = current * (1.0 + correction) / (1.0 + weight)
    return current


def solution(mesh):
    placed = (
        P("brick", None, None, None),
        P("view", "brick", None, None, None),
        P("view", None, None),
        P("view", "brick", None, None),
        P("view", "brick", None),
        P("view", "brick", None),
        P("view", "brick", None),
        P("view", None),
    )
    return jax.shard_map(
        on_device,
        mesh=mesh,
        in_specs=placed,
        out_specs=P("brick", None, None, None),
        check_vma=False,
    )
```

profile of v0, /device:TPU:0, one launch (start us, length us, event | category | flops | bytes accessed | tf_op | source)
XLA Modules:
  0.0 637.1 jit_solution(17363092485871562912)
XLA Ops:
  6.5 1.3 fusion.66
  11.9 2.2 dynamic-slice_convert_fusion.1
  14.1 0.7 copy.56
  15.0 0.7 bitcast_subtract_fusion
  15.8 1.2 gather_fusion.4
  17.0 1.6 gather_fusion.1
  18.8 1.2 gather_fusion.2
  20.1 1.2 gather_fusion.3
  21.7 0.8 gather_fusion.5
  22.4 0.8 gather_fusion
  25.0 1.6 fusion.22
  26.6 1.7 convolution_bitcast_fusion.2
  28.3 2.6 fusion.6
  31.5 3.0 gather_fusion.11
  34.6 10.2 %all-gather.4.cloned.1.call-done = bf16[256,32,128]{2,1,0:T(8,128)(2,1)} async-done(((bf16[32,32,128]{2,1,0:T(8,128)(2,1)}), bf16[256,32,128]{2,1,0:T(8,128)(2,1)}) %all-gather.4.cloned.1.call-update) | async-done | bytes 2097168 | tf_op jit(solution)/shard_map/all_gather | solution.py:142
  44.8 2.3 gather_fusion.9
  47.1 0.9 fusion.20
  48.1 1.7 convolution_bitcast_fusion.4
  49.8 3.1 convert_divide_fusion.1
  52.9 2.0 fusion.10
  54.9 1.7 convolution_bitcast_fusion.3
  56.6 2.6 fusion.8
  59.9 3.0 gather_fusion.10
  62.8 16.0 %select_select_fusion.1 = (f32[256,32,128]{2,1,0:T(8,128)S(1)}, f32[256,32,128]{2,1,0:T(8,128)}) fusion(f32[256,32,128]{2,1,0:T(8,128)} %gather_fusion.11, pred[256]{0:T(512)(128)(4,1)S(1)} %get-tuple-element.12, pred[256]{0:T(512)(128)(4,1)S(1)} %and.102, f32[256,32,128]{2,1,0:T(8,128)} %gather_fusion.10), kind=kLoop, calls=%fused_computation.15 | loop fusion | flops 4194304 | bytes 16777728 | tf_op jit(solution)/shard_map/jit(_where)/select_n | solution.py:123
  78.8 4.3 copy.69
  83.2 4.5 all-to-all-start.1
  87.7 6.5 %copy.64 = f32[8,32,32,128]{3,1,2,0:T(8,128)} copy(f32[8,32,32,128]{3,2,1,0:T(8,128)} %bitcast.133) | data formatting | bytes 8388608 | tf_op jit(solution)/shard_map/reshape | solution.py:124
  94.3 42.6 %all-to-all-done.1 = f32[8,32,32,128]{3,1,2,0:T(8,128)} async-done(((f32[8,32,32,128]{3,1,2,0:T(8,128)}), f32[8,32,32,128]{3,1,2,0:T(8,128)}, u32[]{:S(2)}, u32[]{:S(2)}) %all-to-all-start.1) | async-done | bytes 4194336 | tf_op jit(solution)/shard_map/all_to_all | solution.py:125
  136.8 4.6 all-to-all-start
  141.5 52.0 %all-gather = s32[1,8,32,1]{2,3,0,1:T(1,128)S(1)} all-gather(s32[1,1,32,1]{2,3,0,1:T(1,128)S(1)} %bitcast.124), channel_id=2, replica_groups=mesh['view'=4,'brick'=8] {'brick'}, dimensions={1}, use_global_device_ids=true | all-gather | bytes 1152 | tf_op jit(solution)/shard_map/all_gather | solution.py:63
  194.1 7.9 %all_gather.20 = s32[1,8,32]{2,0,1:T(1,128)S(1)} all-gather(s32[1,1,32]{2,0,1:T(1,128)S(1)} %bitcast.126), channel_id=1, replica_groups=mesh['view'=4,'brick'=8] {'brick'}, dimensions={1}, use_global_device_ids=true | all-gather | bytes 1152 | tf_op jit(solution)/shard_map/all_gather | solution.py:64
  202.0 0.7 gather_fusion.7
  202.8 8.7 %all_gather.21 = s32[1,8,32]{2,0,1:T(1,128)S(1)} all-gather(s32[1,1,32]{2,0,1:T(1,128)S(1)} %bitcast.128), channel_id=1, replica_groups=mesh['view'=4,'brick'=8] {'brick'}, dimensions={1}, use_global_device_ids=true | all-gather | bytes 1152 | tf_op jit(solution)/shard_map/all_gather | solution.py:65
  211.5 0.7 gather_fusion.8
  212.3 7.9 %all_gather.19 = s32[1,8,32]{2,0,1:T(1,128)S(1)} all-gather(s32[1,1,32]{2,0,1:T(1,128)S(1)} %bitcast.117), channel_id=1, replica_groups=mesh['view'=4,'brick'=8] {'brick'}, dimensions={1}, use_global_device_ids=true | all-gather | bytes 1152 | tf_op jit(solution)/shard_map/all_gather | solution.py:66
  220.2 0.7 gather_fusion.6
  221.6 2.8 copy.70
  224.5 1.6 fusion.47
  226.5 2.8 copy.65
  229.3 1.6 fusion.49
  231.5 13.4 %dynamic_update_slice.10 = f32[32,64,256]{2,1,0:T(8,128)S(1)} dynamic-update-slice(f32[32,64,256]{2,1,0:T(8,128)S(1)} %broadcast.183.clone.1, f32[32,32,128]{2,1,0:T(8,128)S(1)} %copy.71, s32[]{:T(128)} %constant.39.clone.1, s32[]{:T(128)S(6)} %select_n.82, s32[]{:T(128)S(6)} %select_n.83) | dynamic-update-slice | bytes 1048580 | tf_op jit(solution)/shard_map/dynamic_update_slice | solution.py:129
  244.9 1.7 broadcast.183.clone
  246.6 13.9 %dynamic_update_slice.9 = f32[32,64,256]{2,1,0:T(8,128)} dynamic-update-slice(f32[32,64,256]{2,1,0:T(8,128)} %broadcast.183.clone, f32[32,32,128]{2,1,0:T(8,128)S(1)} %copy.66, s32[]{:T(128)} %constant.39.clone.1, s32[]{:T(128)S(6)} %select_n.82, s32[]{:T(128)S(6)} %select_n.83) | dynamic-update-slice | bytes 1048580 | tf_op jit(solution)/shard_map/dynamic_update_slice | solution.py:129
  260.6 154.2 %all-reduce.6.cloned.1.call-done = (f32[2,16,64,256]{3,2,1,0:T(8,128)}, f32[2,16,64,256]{3,2,1,0:T(8,128)}) async-done(((f32[2,16,64,256]{3,2,1,0:T(8,128)}, f32[2,16,64,256]{3,2,1,0:T(8,128)}), (f32[2,16,64,256]{3,2,1,0:T(8,128)}, f32[2,16,64,256]{3,2,1,0:T(8,128)})) %all-reduce.6.cloned.1.call-update) | async-done | bytes 4194320 | tf_op jit(solution)/shard_map/psum | solution.py:133
  414.8 3.5 multiply_divide_fusion.1
  418.2 1.3 copy-done.4
  419.5 0.9 dynamic-slice_convert_fusion
  420.7 26.6 %all-gather.6.cloned.1.call-done = bf16[256,32,128]{2,1,0:T(8,128)(2,1)} async-done(((bf16[32,32,128]{2,1,0:T(8,128)(2,1)}), bf16[256,32,128]{2,1,0:T(8,128)(2,1)}) %all-gather.6.cloned.1.call-update) | async-done | bytes 2097168 | tf_op jit(solution)/shard_map/all_gather | solution.py:142
  447.4 2.3 gather_fusion.12
  449.7 0.9 fusion.18
  450.7 1.7 convolution_bitcast_fusion.1
  452.4 2.9 convert_divide_fusion
  455.3 2.0 fusion.2
  457.3 1.7 convolution_bitcast_fusion
  459.0 2.9 fusion
  462.5 3.0 gather_fusion.13
  465.5 3.8 select_select_fusion
  469.2 2.4 copy.78
  471.6 51.6 %all_to_all.15 = f32[8,32,32,128]{3,1,2,0:T(8,128)S(1)} all-to-all(f32[8,32,32,128]{3,1,2,0:T(8,128)S(1)} %copy.78), channel_id=1, replica_groups=mesh['view'=4,'brick'=8] {'brick'}, dimensions={0} | all-to-all | bytes 8388608 | tf_op jit(solution)/shard_map/all_to_all | solution.py:125
  523.8 1.6 fusion.45
  525.8 1.5 broadcast.183
  527.3 14.1 %dynamic_update_slice.11 = f32[32,64,256]{2,1,0:T(8,128)} dynamic-update-slice(f32[32,64,256]{2,1,0:T(8,128)} %broadcast.183, f32[32,32,128]{2,1,0:T(8,128)S(1)} %copy.80, s32[]{:T(128)} %constant.39.clone.1, s32[]{:T(128)S(6)} %select_n.82, s32[]{:T(128)S(6)} %select_n.83) | dynamic-update-slice | bytes 1048580 | tf_op jit(solution)/shard_map/dynamic_update_slice | solution.py:129
  541.4 84.5 %all-reduce.4.cloned.1.call-done = f32[2,16,64,256]{3,2,1,0:T(8,128)} async-done(((f32[2,16,64,256]{3,2,1,0:T(8,128)}), f32[2,16,64,256]{3,2,1,0:T(8,128)}) %all-reduce.4.cloned.1.call-update) | async-done | bytes 2097168 | tf_op jit(solution)/shard_map/psum | solution.py:133
  625.9 4.2 multiply_divide_fusion
  (85 shorter events, 8.0 us)
Async XLA Ops:
  6.5 12.1 %copy-start.1 = (s32[1,1,32,1]{2,3,1,0:T(1,128)S(1)}, s32[1,1,32,1]{2,3,1,0:T(1,128)}, u32[]{:S(2)}) copy-start(s32[1,1,32,1]{2,3,1,0:T(1,128)} %param.17) | copy-start | bytes 388
  6.5 12.3 %copy-start.2 = (s32[1,1,32]{2,1,0:T(1,128)S(1)}, s32[1,1,32]{2,1,0:T(1,128)}, u32[]{:S(2)}) copy-start(s32[1,1,32]{2,1,0:T(1,128)} %param.18) | copy-start | bytes 388
  6.5 13.5 %copy-start.3 = (s32[1,1,32]{2,1,0:T(1,128)S(1)}, s32[1,1,32]{2,1,0:T(1,128)}, u32[]{:S(2)}) copy-start(s32[1,1,32]{2,1,0:T(1,128)} %param.19) | copy-start | bytes 388
  6.5 38.2 %all-gather.4.cloned.1.call-start = ((), (), s32[]{:S(2)}) async-start(), calls=%async_computation.3 | async-start | bytes 2359296 | tf_op jit(solution)/shard_map/all_gather | solution.py:142
  21.6 0.8 copy-start
  22.4 1.6 copy-start.7
  48.1 1.7 copy-start.8
  83.2 53.6 %all-to-all-start.1 = ((f32[8,32,32,128]{3,1,2,0:T(8,128)}), f32[8,32,32,128]{3,1,2,0:T(8,128)}, u32[]{:S(2)}, u32[]{:S(2)}) async-start(f32[8,32,32,128]{3,1,2,0:T(8,128)} %copy.69), calls=%async_computation.1 | async-start | bytes 8388608 | tf_op jit(solution)/shard_map/all_to_all | solution.py:125
  136.8 89.6 %all-to-all-start = ((f32[8,32,32,128]{3,1,2,0:T(8,128)}), f32[8,32,32,128]{3,1,2,0:T(8,128)}, u32[]{:S(2)}, u32[]{:S(2)}) async-start(f32[8,32,32,128]{3,1,2,0:T(8,128)} %copy.64), calls=%async_computation | async-start | bytes 8388608 | tf_op jit(solution)/shard_map/all_to_all | solution.py:125
  141.4 273.3 %all-reduce.6.cloned.1.call-start = ((), (), s32[]{:S(2)}) async-start(), calls=%async_computation.6 | async-start | bytes 8388608 | tf_op jit(solution)/shard_map/psum | solution.py:133
  244.9 15.6 %copy-start.6 = (f32[32,64,256]{2,1,0:T(8,128)}, f32[32,64,256]{2,1,0:T(8,128)S(1)}, u32[]{:S(2)}) copy-start(f32[32,64,256]{2,1,0:T(8,128)S(1)} %dynamic_update_slice.10) | copy-start | bytes 6291460
  260.5 186.9 %all-gather.6.cloned.1.call-start = ((), (), s32[]{:S(2)}) async-start(), calls=%async_computation.4 | async-start | bytes 2359296 | tf_op jit(solution)/shard_map/all_gather | solution.py:142
  418.2 1.3 copy-start.4
  420.5 205.4 %all-reduce.4.cloned.1.call-start = ((), (), s32[]{:S(2)}) async-start(), calls=%async_computation.5 | async-start | bytes 4194304 | tf_op jit(solution)/shard_map/psum | solution.py:133
  450.7 1.7 copy-start.9
  527.3 98.5 %copy-start.5 = (f32[2,16,64,256]{3,2,1,0:T(8,128)S(1)}, f32[2,16,64,256]{3,2,1,0:T(8,128)}, u32[]{:S(2)}) copy-start(f32[2,16,64,256]{3,2,1,0:T(8,128)} %copy-done.4) | copy-start | bytes 6291460
Sparse Core Ops, SparseCore 0:
  14.2 30.5 all-gather.3
  260.6 154.0 all-reduce.5
  420.6 26.7 all-gather.5
  541.5 84.2 all-reduce.3
where the time goes:
time: 648 us; the launch traced here: 637 us
  waiting for transfers between devices  318 us (49%)
  blocking collectives  128 us (20%)
  local copies, waits for them, and re-layouts  97.2 us (15%)
  matrix products  35 us (5%)
  other arithmetic  31.1 us (5%)
  between operations  18.1 us (3%)
  starting transfers between devices  9.48 us (1%)
    psum x2, waiting for transfers between devices, to_owners(): return lax.psum(brick_part, 'view')  239 us
    all_gather x1, blocking collectives, on_device(): lax.all_gather(seg_owner[:, :, :, 0], 'brick', axis=1, tiled=True)  52 us
    all_to_all x1, blocking collectives, to_owners(): lax.all_to_all(outgoing, 'brick', split_axis=0, concat_axis=0, tiled=True)  51.6 us
    all_to_all x2, waiting for transfers between devices, to_owners(): lax.all_to_all(outgoing, 'brick', split_axis=0, concat_axis=0, tiled=True)  42.6 us
    dynamic_update_slice x3, local copies, waits for them, and re-layouts, to_owners(): lax.dynamic_update_slice(jnp.zeros((own_rows, brick_y, brick_z), jnp.floa...  41.3 us
    all_gather x2, waiting for transfers between devices, on_device(): gathered = lax.all_gather(cropped, 'brick', axis=0, tiled=True)  36.9 us
    select_n x2, other arithmetic, to_owners(): jnp.where(back_mask[:, None, None], jnp.take(projected, back_rows, axis=0...  19.7 us
    dot_general x5, matrix products, apply_blur(): volume = jnp.einsum('...xyz,xw->...wyz', volume, along_x, precision=highest)  14.2 us
  transfers between devices with their start and end apart: 6, of which 5 were waited for; matrix products, arithmetic and copies ran while one was open for 6% of the time, Pallas kernels for 0%

commit v1 on v0

--- a/solution.py
+++ b/solution.py
@@ -5,6 +5,11 @@
 
 ITERS = 2
 EXTMAX = 4
+
+
+def add_all(x, axis):
+    parts = lax.all_gather(x, axis)
+    return jnp.sum(parts, axis=0)
 
 
 def blur_matrix(tap_values, length):
@@ -130,7 +135,7 @@
             jnp.zeros((own_rows, brick_y, brick_z), jnp.float32), accumulated, (0, shift_y, shift_z)
         )
         brick_part = brick_part.reshape(per_owner, brick_x, brick_y, brick_z)
-        return lax.psum(brick_part, "view")
+        return add_all(brick_part, "view")
 
     weight = to_owners(apply_blur(jnp.ones((tile_x, tile_y, tile_z), jnp.float32), backward))
     current = estimate

time: 648 us -> 788 us (1.22)
  waiting for transfers between devices: 318 us -> 403 us
  blocking collectives: 128 us -> 180 us
  other arithmetic: 31.1 us -> 41.3 us
    all_gather x0 -> x3, waiting for transfers between devices: none -> 368 us  [add_all(): parts = lax.all_gather(x, axis)]
    psum x2 -> x0, waiting for transfers between devices: 239 us -> none  [to_owners(): return lax.psum(brick_part, 'view')]
    all_to_all x1 -> x2, blocking collectives: 51.6 us -> 103 us  [to_owners(): lax.all_to_all(outgoing, 'brick', split_axis=0, concat_axis=0, tiled=True)]
    all_to_all x2 -> x1, waiting for transfers between devices: 42.6 us -> 0.01 us  [to_owners(): lax.all_to_all(outgoing, 'brick', split_axis=0, concat_axis=0, tiled=True)]
    reduce_sum x0 -> x3, other arithmetic: none -> 15.9 us  [add_all(): return jnp.sum(parts, axis=0)]
    select_n x2, other arithmetic: 19.7 us -> 9.95 us  [to_owners(): jnp.where(back_mask[:, None, None], jnp.take(projected, back_rows, axis=0...]
where the time goes in v1:
time: 788 us; the launch traced here: 777 us
  waiting for transfers between devices  403 us (51%)
  blocking collectives  180 us (23%)
  local copies, waits for them, and re-layouts  95.8 us (12%)
  other arithmetic  41.3 us (5%)
  matrix products  34.5 us (4%)
  between operations  18.2 us (2%)
    all_gather x3, waiting for transfers between devices, add_all(): parts = lax.all_gather(x, axis)  368 us
    all_to_all x2, blocking collectives, to_owners(): lax.all_to_all(outgoing, 'brick', split_axis=0, concat_axis=0, tiled=True)  103 us
    all_gather x1, blocking collectives, on_device(): lax.all_gather(seg_owner[:, :, :, 0], 'brick', axis=1, tiled=True)  51.9 us
    dynamic_update_slice x3, local copies, waits for them, and re-layouts, to_owners(): lax.dynamic_update_slice(jnp.zeros((own_rows, brick_y, brick_z), jnp.floa...  40.1 us
    all_gather x2, waiting for transfers between devices, on_device(): gathered = lax.all_gather(cropped, 'brick', axis=0, tiled=True)  34.8 us
    reduce_sum x3, other arithmetic, add_all(): return jnp.sum(parts, axis=0)  15.9 us
  transfers between devices with their start and end apart: 6, of which 5 were waited for; matrix products, arithmetic and copies ran while one was open for 6% of the time, Pallas kernels for 0%

profile of v1, /device:TPU:0, one launch (start us, length us, event | category | flops | bytes accessed | tf_op | source)
XLA Modules:
  0.0 777.3 jit_solution(4650851245382766486)
XLA Ops:
  6.5 1.3 fusion.70
  11.9 2.2 dynamic-slice_convert_fusion
  15.8 1.2 gather_fusion.4
  17.0 1.6 gather_fusion.1
  18.6 0.9 convert_reduce_fusion.2
  20.2 1.2 gather_fusion.2
  21.4 1.2 gather_fusion.3
  23.8 0.8 gather_fusion
  26.3 1.6 fusion.26
  27.9 1.7 convolution_bitcast_fusion.2
  29.6 2.6 fusion.10
  32.9 3.0 gather_fusion.11
  35.9 8.9 %all-gather.7.cloned.1.call-done = bf16[256,32,128]{2,1,0:T(8,128)(2,1)} async-done(((bf16[32,32,128]{2,1,0:T(8,128)(2,1)}), bf16[256,32,128]{2,1,0:T(8,128)(2,1)}) %all-gather.7.cloned.1.call-update) | async-done | bytes 2097168 | tf_op jit(solution)/shard_map/all_gather | solution.py:147
  44.8 2.3 gather_fusion.9
  47.1 0.9 fusion.24
  48.1 1.7 convolution_bitcast_fusion.4
  49.8 3.1 convert_divide_fusion.1
  52.9 2.0 fusion.14
  54.9 1.7 convolution_bitcast_fusion.3
  56.5 2.6 fusion.12
  59.8 3.0 gather_fusion.10
  62.8 6.2 select_select_fusion.1
  68.9 4.3 copy.71
  73.3 4.7 all-to-all-start.1
  78.1 51.9 %all-gather = s32[1,8,32,1]{2,3,0,1:T(1,128)S(1)} all-gather(s32[1,1,32,1]{2,3,0,1:T(1,128)S(1)} %bitcast.124), channel_id=2, replica_groups=mesh['view'=4,'brick'=8] {'brick'}, dimensions={1}, use_global_device_ids=true | all-gather | bytes 1152 | tf_op jit(solution)/shard_map/all_gather | solution.py:68
  130.6 7.9 %all_gather.29 = s32[1,8,32]{2,0,1:T(1,128)S(1)} all-gather(s32[1,1,32]{2,0,1:T(1,128)S(1)} %bitcast.126), channel_id=1, replica_groups=mesh['view'=4,'brick'=8] {'brick'}, dimensions={1}, use_global_device_ids=true | all-gather | bytes 1152 | tf_op jit(solution)/shard_map/all_gather | solution.py:69
  139.3 8.7 %all_gather.30 = s32[1,8,32]{2,0,1:T(1,128)S(1)} all-gather(s32[1,1,32]{2,0,1:T(1,128)S(1)} %bitcast.128), channel_id=1, replica_groups=mesh['view'=4,'brick'=8] {'brick'}, dimensions={1}, use_global_device_ids=true | all-gather | bytes 1152 | tf_op jit(solution)/shard_map/all_gather | solution.py:70
  148.8 7.9 %all_gather.28 = s32[1,8,32]{2,0,1:T(1,128)S(1)} all-gather(s32[1,1,32]{2,0,1:T(1,128)S(1)} %bitcast.117), channel_id=1, replica_groups=mesh['view'=4,'brick'=8] {'brick'}, dimensions={1}, use_global_device_ids=true | all-gather | bytes 1152 | tf_op jit(solution)/shard_map/all_gather | solution.py:71
  158.2 2.8 copy.72
  161.1 1.6 fusion.51
  163.3 13.4 %dynamic_update_slice.10 = f32[32,64,256]{2,1,0:T(8,128)S(1)} dynamic-update-slice(f32[32,64,256]{2,1,0:T(8,128)S(1)} %broadcast.183.clone.1, f32[32,32,128]{2,1,0:T(8,128)S(1)} %copy.73, s32[]{:T(128)} %constant.39.clone.1, s32[]{:T(128)S(6)} %select_n.82, s32[]{:T(128)S(6)} %select_n.83) | dynamic-update-slice | bytes 1048580 | tf_op jit(solution)/shard_map/dynamic_update_slice | solution.py:134
  176.6 1.3 copy-done.8
  178.1 4.6 copy.64
  182.6 51.7 %all_to_all.15 = f32[8,32,32,128]{3,1,2,0:T(8,128)S(1)} all-to-all(f32[8,32,32,128]{3,1,2,0:T(8,128)S(1)} %copy.64), channel_id=1, replica_groups=mesh['view'=4,'brick'=8] {'brick'}, dimensions={0} | all-to-all | bytes 8388608 | tf_op jit(solution)/shard_map/all_to_all | solution.py:130
  235.0 1.6 fusion.53
  237.2 13.4 %dynamic_update_slice.9 = f32[32,64,256]{2,1,0:T(8,128)S(1)} dynamic-update-slice(f32[32,64,256]{2,1,0:T(8,128)S(1)} %broadcast.183.clone, f32[32,32,128]{2,1,0:T(8,128)S(1)} %copy.66, s32[]{:T(128)} %constant.39.clone.1, s32[]{:T(128)S(6)} %select_n.82, s32[]{:T(128)S(6)} %select_n.83) | dynamic-update-slice | bytes 1048580 | tf_op jit(solution)/shard_map/dynamic_update_slice | solution.py:134
  250.6 1.3 copy-done.9
  252.0 74.9 %all-gather.11.cloned.1.call-done = f32[4,2,16,64,256]{4,3,2,1,0:T(8,128)} async-done(((f32[1,2,16,64,256]{4,3,2,1,0:T(8,128)}), f32[4,2,16,64,256]{4,3,2,1,0:T(8,128)}) %all-gather.11.cloned.1.call-update) | async-done | bytes 8388624 | tf_op jit(solution)/shard_map/all_gather | solution.py:11
  326.8 4.4 reduce_sum.121
  331.3 145.0 %all-gather.9.cloned.1.call-done = f32[4,2,16,64,256]{4,3,2,1,0:T(8,128)} async-done(((f32[1,2,16,64,256]{4,3,2,1,0:T(8,128)}), f32[4,2,16,64,256]{4,3,2,1,0:T(8,128)}) %all-gather.9.cloned.1.call-update) | async-done | bytes 8388624 | tf_op jit(solution)/shard_map/all_gather | solution.py:11
  476.2 5.7 reduce_sum.120
  482.0 5.7 fusion.3
  487.7 1.3 copy-done.6
  489.2 0.8 copy.138
  490.3 25.9 %all-gather.13.cloned.1.call-done = bf16[256,32,128]{2,1,0:T(8,128)(2,1)} async-done(((bf16[32,32,128]{2,1,0:T(8,128)(2,1)}), bf16[256,32,128]{2,1,0:T(8,128)(2,1)}) %all-gather.13.cloned.1.call-update) | async-done | bytes 2097168 | tf_op jit(solution)/shard_map/all_gather | solution.py:147
  516.1 2.3 gather_fusion.12
  518.5 0.9 fusion.22
  519.4 1.7 convolution_bitcast_fusion.1
  521.1 2.9 convert_divide_fusion
  524.0 2.0 fusion.6
  526.0 1.7 convolution_bitcast_fusion
  527.7 2.6 fusion.4
  530.3 0.8 copy.81
  531.1 3.0 gather_fusion.13
  534.1 3.8 select_select_fusion
  537.9 2.4 copy.82
  540.3 51.6 %all_to_all.16 = f32[8,32,32,128]{3,1,2,0:T(8,128)S(1)} all-to-all(f32[8,32,32,128]{3,1,2,0:T(8,128)S(1)} %copy.82), channel_id=1, replica_groups=mesh['view'=4,'brick'=8] {'brick'}, dimensions={0} | all-to-all | bytes 8388608 | tf_op jit(solution)/shard_map/all_to_all | solution.py:130
  592.5 1.6 fusion.49
  594.7 13.4 %dynamic_update_slice.11 = f32[32,64,256]{2,1,0:T(8,128)S(1)} dynamic-update-slice(f32[32,64,256]{2,1,0:T(8,128)S(1)} %broadcast.183, f32[32,32,128]{2,1,0:T(8,128)S(1)} %copy.84, s32[]{:T(128)} %constant.39.clone.1, s32[]{:T(128)S(6)} %select_n.82, s32[]{:T(128)S(6)} %select_n.83) | dynamic-update-slice | bytes 1048580 | tf_op jit(solution)/shard_map/dynamic_update_slice | solution.py:134
  608.1 1.3 copy-done.7
  609.4 147.9 %all-gather.15.cloned.1.call-done = f32[4,2,16,64,256]{4,3,2,1,0:T(8,128)} async-done(((f32[1,2,16,64,256]{4,3,2,1,0:T(8,128)}), f32[4,2,16,64,256]{4,3,2,1,0:T(8,128)}) %all-gather.15.cloned.1.call-update) | async-done | bytes 8388624 | tf_op jit(solution)/shard_map/all_gather | solution.py:11
  757.3 5.7 reduce_sum.122
  763.0 4.7 fusion.1
  767.8 2.5 copy.86
  (98 shorter events, 13.5 us)
Async XLA Ops:
  6.5 13.7 %copy-start.2 = (s32[1,1,32]{2,1,0:T(1,128)S(1)}, s32[1,1,32]{2,1,0:T(1,128)}, u32[]{:S(2)}) copy-start(s32[1,1,32]{2,1,0:T(1,128)} %param.18) | copy-start | bytes 388
  6.5 14.9 %copy-start.3 = (s32[1,1,32]{2,1,0:T(1,128)S(1)}, s32[1,1,32]{2,1,0:T(1,128)}, u32[]{:S(2)}) copy-start(s32[1,1,32]{2,1,0:T(1,128)} %param.19) | copy-start | bytes 388
  6.5 38.2 %all-gather.7.cloned.1.call-start = ((), (), s32[]{:S(2)}) async-start(), calls=%async_computation.3 | async-start | bytes 2359296 | tf_op jit(solution)/shard_map/all_gather | solution.py:147
  23.0 0.8 copy-start
  23.8 1.6 copy-start.10
  48.1 1.7 copy-start.11
  73.3 4.7 copy-start.1
  73.3 84.9 %all-to-all-start.1 = ((f32[8,32,32,128]{3,1,2,0:T(8,128)}), f32[8,32,32,128]{3,1,2,0:T(8,128)}, u32[]{:S(2)}, u32[]{:S(2)}) async-start(f32[8,32,32,128]{3,1,2,0:T(8,128)} %copy.71), calls=%async_computation.1 | async-start | bytes 8388608 | tf_op jit(solution)/shard_map/all_to_all | solution.py:130
  78.0 248.8 %all-gather.11.cloned.1.call-start = ((), (), s32[]{:S(2)}) async-start(), calls=%async_computation.5 | async-start | bytes 10485760 | tf_op jit(solution)/shard_map/all_gather | solution.py:11
  176.6 1.4 copy-start.8
  178.0 298.2 %all-gather.9.cloned.1.call-start = ((), (), s32[]{:S(2)}) async-start(), calls=%async_computation.4 | async-start | bytes 10485760 | tf_op jit(solution)/shard_map/all_gather | solution.py:11
  250.6 1.3 copy-start.9
  251.9 264.2 %all-gather.13.cloned.1.call-start = ((), (), s32[]{:S(2)}) async-start(), calls=%async_computation.6 | async-start | bytes 2359296 | tf_op jit(solution)/shard_map/all_gather | solution.py:147
  331.2 150.7 %copy-start.4 = (f32[2,16,64,256]{3,2,1,0:T(8,128)}, f32[2,16,64,256]{3,2,1,0:T(8,128)S(1)}, u32[]{:S(2)}) copy-start(f32[2,16,64,256]{3,2,1,0:T(8,128)S(1)} %reduce_sum.121) | copy-start | bytes 6291460
  487.7 1.3 copy-start.6
  490.0 267.3 %all-gather.15.cloned.1.call-start = ((), (), s32[]{:S(2)}) async-start(), calls=%async_computation.7 | async-start | bytes 10485760 | tf_op jit(solution)/shard_map/all_gather | solution.py:11
  519.4 1.7 copy-start.12
  608.1 1.3 copy-start.7
  609.4 153.6 %copy-start.5 = (f32[2,16,64,256]{3,2,1,0:T(8,128)S(1)}, f32[2,16,64,256]{3,2,1,0:T(8,128)}, u32[]{:S(2)}) copy-start(f32[2,16,64,256]{3,2,1,0:T(8,128)} %copy-done.4) | copy-start | bytes 6291460
Sparse Core Ops, SparseCore 0:
  14.2 30.4 all-gather.6
  178.1 148.6 all-gather.10
  328.4 147.7 all-gather.8
  490.1 25.9 all-gather.12
  609.5 147.7 all-gather.14
